TPU v7x, 128 devices: a whole 4x4x4 slice. The times are simulated.
128 devices in a mesh: expert: 32 (over y, x, core), dp: 4 (over z).
Axes of the slice: x: 4, y: 4, z: 4, core: 2. Of those that a mesh axis runs over, the one named last changes fastest.
Arguments:
- tokens: bfloat16 [4096, 4096], P('expert', 'dp'), may hold values from -6 to 6
- cotangent: bfloat16 [4096, 4096], P('expert', 'dp'), may hold values from -6 to 6
- gate_probs: bfloat16 [4096, 8], P('expert'), may hold values from 0.019897461 to 0.3984375
- expert_ids: int32 [4096, 8], P('expert'), may hold values from 0 to 31, all different within a row; in each aligned block of 128 rows (0 to 127, 128 to 255, ...) at most 36 rows name the same one
- gate_weight: bfloat16 [32, 4096, 1024], P('expert', 'dp'), may hold values from -0.09375 to 0.09375
- up_weight: bfloat16 [32, 4096, 1024], P('expert', 'dp'), may hold values from -0.09375 to 0.09375
- down_weight: bfloat16 [32, 1024, 4096], P('expert', None, 'dp'), may hold values from -0.1875 to 0.1875
Outputs:
- grad_tokens: bfloat16 [4096, 4096], P('expert', 'dp')
- grad_gates: float32 [4096, 8], P('expert')
- grad_gate_weight: float32 [32, 4096, 1024], P('expert', 'dp')
- grad_up_weight: float32 [32, 4096, 1024], P('expert', 'dp')
- grad_down_weight: float32 [32, 1024, 4096], P('expert', None, 'dp')
Inputs may be any that keep to these rules, and one draw needn't show every extreme that they name: `expert_ids`: each row names 8 different experts. Among the 128 rows of one group no expert is named more than 36 times, and in every draw some expert is named exactly 36 times by the rows of some group.
All inputs are finite; a program needn't handle non-finite values.
Results may differ from a plain program's by a relative error of at most 0.012.
Values may be sent and summed in bfloat16 or wider, within the bound.
A program may use at most 128 MiB of HBM per device.

v0:
```python
import jax
import jax.numpy as jnp
from jax import lax
from jax.sharding import PartitionSpec as P

TOP = 8
EXPERTS = 32
CAP = 36


def local_slots(expert_ids):
    flat_ids = expert_ids.reshape(-1)
    columns = jnp.arange(EXPERTS, dtype=jnp.int32)
    member = (flat_ids[:, None] == columns[None, :]).astype(jnp.int32)
    ranked = jnp.cumsum(member, axis=0) - 1
    within = jnp.sum(member * ranked, axis=1)
    return flat_ids * CAP + within


def pack_rows(tokens, cotangent, gate_probs, target):
    token_count = tokens.shape[0]
    slot_total = EXPERTS * CAP
    slot_index = jnp.arange(slot_total, dtype=jnp.int32)
    placed = target[None, :] == slot_index[:, None]
    chosen = jnp.any(placed.reshape(slot_total, token_count, TOP), axis=2).astype(jnp.bfloat16)
    x_send = jnp.dot(chosen, tokens, preferred_element_type=jnp.float32).astype(jnp.bfloat16)
    dy_send = jnp.dot(chosen, cotangent, preferred_element_type=jnp.float32).astype(jnp.bfloat16)
    weights_flat = gate_probs.reshape(-1).astype(jnp.float32)
    g_send = jnp.sum(jnp.where(placed, weights_flat[None, :], 0.0), axis=1).astype(jnp.bfloat16)
    return (x_send, dy_send, g_send)


def hidden_units(gate_pre, up_pre, back_hidden, g_rows):
    sigmoid_gate = jax.nn.sigmoid(gate_pre)
    swish_gate = gate_pre * sigmoid_gate
    hidden = (swish_gate * up_pre).astype(jnp.bfloat16)
    product = back_hidden * hidden.astype(jnp.float32)
    grad_hidden = g_rows * back_hidden
    derivative = sigmoid_gate * (1.0 + gate_pre * (1.0 - sigmoid_gate))
    grad_gate_pre = (grad_hidden * up_pre * derivative).astype(jnp.bfloat16)
    grad_up_pre = (grad_hidden * swish_gate).astype(jnp.bfloat16)
    return (hidden, grad_gate_pre, grad_up_pre, product)


def shards(tokens, cotangent, gate_probs, expert_ids, gate_weight, up_weight, down_weight):
    expert_count = lax.axis_size("expert")
    data_count = lax.axis_size("dp")
    local_count = gate_weight.shape[0]
    width_part = tokens.shape[1]
    token_count = tokens.shape[0]
    target = local_slots(expert_ids)
    x_send, dy_send, g_send = pack_rows(tokens, cotangent, gate_probs, target)
    x_recv, dy_recv, g_recv = (
        lax.all_to_all(x_send, "expert", split_axis=0, concat_axis=0, tiled=True),
        lax.all_to_all(dy_send, "expert", split_axis=0, concat_axis=0, tiled=True),
        lax.all_to_all(g_send, "expert", split_axis=0, concat_axis=0, tiled=True),
    )
    x_grid = x_recv.reshape(expert_count, local_count, CAP, width_part)
    dy_grid = dy_recv.reshape(expert_count, local_count, CAP, width_part)
    g_grid = g_recv.reshape(expert_count, local_count, CAP)
    g_rows = jnp.transpose(g_grid, (1, 0, 2)).astype(jnp.float32)[..., None]
    gate_part = jnp.einsum(
        "secd,edf->escf", x_grid, gate_weight, preferred_element_type=jnp.float32
    )
    up_part = jnp.einsum("secd,edf->escf", x_grid, up_weight, preferred_element_type=jnp.float32)
    back_part = jnp.einsum(
        "secd,efd->escf", dy_grid, down_weight, preferred_element_type=jnp.float32
    )
    gate_pre, up_pre, back_hidden = (
        lax.psum_scatter(gate_part, "dp", scatter_dimension=3, tiled=True),
        lax.psum_scatter(up_part, "dp", scatter_dimension=3, tiled=True),
        lax.psum_scatter(back_part, "dp", scatter_dimension=3, tiled=True),
    )
    hidden, grad_gate_pre, grad_up_pre, product = hidden_units(
        gate_pre, up_pre, back_hidden, g_rows
    )
    block_sum = jnp.sum(product, axis=3, keepdims=True).astype(jnp.bfloat16)
    hidden_all, gate_grad_all, up_grad_all, gate_blocks = (
        lax.all_gather(hidden, "dp", axis=3, tiled=True),
        lax.all_gather(grad_gate_pre, "dp", axis=3, tiled=True),
        lax.all_gather(grad_up_pre, "dp", axis=3, tiled=True),
        lax.all_gather(block_sum, "dp", axis=3, tiled=True),
    )
    input_terms = jnp.einsum(
        "escf,edf->secd", gate_grad_all, gate_weight, preferred_element_type=jnp.float32
    )
    input_terms = input_terms + jnp.einsum(
        "escf,edf->secd", up_grad_all, up_weight, preferred_element_type=jnp.float32
    )
    input_part = input_terms.astype(jnp.bfloat16).reshape(
        expert_count * local_count * CAP, width_part
    )
    scaled_dy = dy_grid * g_grid[..., None]
    grad_down = jnp.einsum(
        "escf,secd->efd", hidden_all, scaled_dy, preferred_element_type=jnp.float32
    )
    grad_gate = jnp.einsum(
        "secd,escf->edf", x_grid, gate_grad_all, preferred_element_type=jnp.float32
    )
    grad_up = jnp.einsum("secd,escf->edf", x_grid, up_grad_all, preferred_element_type=jnp.float32)
    block_send = jnp.transpose(gate_blocks, (1, 0, 2, 3)).reshape(
        expert_count * local_count * CAP, data_count
    )
    input_table, gate_table = (
        lax.all_to_all(input_part, "expert", split_axis=0, concat_axis=0, tiled=True),
        lax.all_to_all(block_send, "expert", split_axis=0, concat_axis=0, tiled=True),
    )
    picked = jnp.take(input_table, target, axis=0).astype(jnp.float32)
    grad_tokens = picked.reshape(token_count, TOP, width_part).sum(1).astype(jnp.bfloat16)
    grad_gates = (
        jnp.take(gate_table, target, axis=0).astype(jnp.float32).sum(1).reshape(token_count, TOP)
    )
    return (grad_tokens, grad_gates, grad_gate, grad_up, grad_down)


def solution(mesh):
    placed = (
        P("expert", "dp"),
        P("expert", "dp"),
        P("expert", None),
        P("expert", None),
        P("expert", "dp", None),
        P("expert", "dp", None),
        P("expert", None, "dp"),
    )
    return jax.shard_map(
        shards,
        mesh=mesh,
        in_specs=placed,
        out_specs=(
            P("expert", "dp"),
            P("expert", None),
            P("expert", "dp", None),
            P("expert", "dp", None),
            P("expert", None, "dp"),
        ),
        check_vma=False,
    )
```

profile of v0, /device:TPU:0, one launch (start us, length us, event | category | flops | bytes accessed | tf_op | source)
XLA Modules:
  0.0 406.6 jit_solution(17590556254104163297)
XLA Ops:
  7.2 0.9 copy.58
  8.4 9.0 %reduce-window.6 = s32[32,8,128]{2,1,0:T(8,128)S(1)} reduce-window(s32[32,8,128]{2,1,0:T(8,128)S(1)} %fusion.37, s32[]{:T(128)} %constant.25.clone.1), window={size=1x1x128 pad=0_0x0_0x127_0}, to_apply=%region_0.0 | reduce-window | flops 4161536 | bytes 262148 | tf_op jit(solution)/shard_map/reduce-window
  17.5 0.1 copy.60
  18.0 0.7 compare_and_fusion.1
  18.7 4.2 %fusion = pred[1152,128]{1,0:T(8,128)(4,1)S(1)} fusion(s32[128,8]{0,1:T(8,128)S(1)} %get-tuple-element.35), kind=kLoop, calls=%fused_computation.6 | loop fusion | flops 2211840 | bytes 151552 | tf_op jit(solution)/shard_map/reduce_or | solution.py:25
  22.9 3.1 convolution_convert_fusion
  26.0 4.1 all_to_all.33
  30.1 41.6 %all_to_all.45 = bf16[32,36,1024]{2,1,0:T(8,128)(2,1)S(1)} all-to-all(bf16[32,36,1024]{2,1,0:T(8,128)(2,1)} %all_to_all.33), channel_id=1, replica_groups=mesh['expert'=32,'dp'=4] {'expert'}, dimensions={0} | all-to-all | bytes 4718592 | tf_op jit(solution)/shard_map/all_to_all | solution.py:54
  71.7 1.5 copy-done.2
  73.2 4.6 %convolution_bitcast_fusion.1 = f32[1,32,36,1024]{3,2,1,0:T(8,128)} fusion(bf16[32,36,1024]{2,1,0:T(8,128)(2,1)S(1)} %all_to_all.45, bf16[1,1024,1024]{2,1,0:T(8,128)(2,1)S(1)} %copy-done), kind=kOutput, calls=%fused_computation.21 | convolution fusion | flops 2415919104 | bytes 9175040 | tf_op jit(solution)/shard_map/secd,edf->escf/dot_general | solution.py:65
  77.9 7.6 %convolution_bitcast_fusion = f32[1,32,36,1024]{3,2,1,0:T(8,128)} fusion(bf16[32,36,1024]{2,1,0:T(8,128)(2,1)} %copy-done.2, bf16[1,1024,1024]{2,1,0:T(8,128)(2,1)} %param.11), kind=kOutput, calls=%fused_computation.20 | convolution fusion | flops 2415919104 | bytes 9175040 | tf_op jit(solution)/shard_map/secd,edf->escf/dot_general | solution.py:62
  85.6 1.0 copy-done.5
  86.5 2.2 convolution_convert_fusion.1
  88.7 4.1 all_to_all.31
  92.8 38.4 %all_to_all.46 = bf16[32,36,1024]{2,1,0:T(8,128)(2,1)S(1)} all-to-all(bf16[32,36,1024]{2,1,0:T(8,128)(2,1)} %all_to_all.31), channel_id=1, replica_groups=mesh['expert'=32,'dp'=4] {'expert'}, dimensions={0} | all-to-all | bytes 4718592 | tf_op jit(solution)/shard_map/all_to_all | solution.py:55
  131.2 1.5 copy-done.4
  132.7 4.7 %convolution_bitcast_fusion.2 = f32[1,32,36,1024]{3,2,1,0:T(8,128)} fusion(bf16[32,36,1024]{2,1,0:T(8,128)(2,1)S(1)} %all_to_all.46, bf16[1,1024,1024]{2,1,0:T(8,128)(2,1)S(1)} %copy-done.9), kind=kOutput, calls=%fused_computation.22 | convolution fusion | flops 2415919104 | bytes 9175040 | tf_op jit(solution)/shard_map/secd,efd->escf/dot_general | solution.py:66
  137.5 0.6 copy-done.7
  138.3 0.6 select_reduce_fusion
  139.0 10.7 %all_to_all.47 = bf16[32,36,1]{1,2,0:T(2,128)(2,1)S(1)} all-to-all(bf16[32,36,1]{1,2,0:T(2,128)(2,1)S(1)} %convert_element_type.99), channel_id=1, replica_groups=mesh['expert'=32,'dp'=4] {'expert'}, dimensions={0} | all-to-all | bytes 4608 | tf_op jit(solution)/shard_map/all_to_all | solution.py:56
  149.7 40.1 %reduce-scatter.8.cloned.1.call-done = f32[1,32,36,256]{3,2,1,0:T(8,128)} async-done(((f32[1,32,36,1024]{3,2,1,0:T(8,128)}), f32[1,32,36,256]{3,2,1,0:T(8,128)}) %reduce-scatter.8.cloned.1.call-update) | async-done | bytes 1179664 | tf_op jit(solution)/shard_map/reduce_scatter | solution.py:70
  189.9 57.6 %reduce-scatter.4.cloned.1.call-done = f32[1,32,36,256]{3,2,1,0:T(8,128)} async-done(((f32[1,32,36,1024]{3,2,1,0:T(8,128)}), f32[1,32,36,256]{3,2,1,0:T(8,128)}) %reduce-scatter.4.cloned.1.call-update) | async-done | bytes 1179664 | tf_op jit(solution)/shard_map/reduce_scatter | solution.py:72
  247.5 4.3 %multiply_reduce_fusion = (bf16[32,36]{1,0:T(8,128)(2,1)S(1)}, bf16[1,32,36,256]{3,2,1,0:T(8,128)(2,1)}, bf16[1,32,36,256]{3,2,1,0:T(8,128)(2,1)}, bf16[1,32,36,256]{3,2,1,0:T(8,128)(2,1)}) fusion(f32[1,32,36,256]{3,2,1,0:T(8,128)} %reduce-scatter.4.cloned.1.call-done, f32[1,32,36,256]{3,2,1,0:T(8,128)} %reduce-scatter.6.cloned.1.call-done, ...), kind=kLoop, calls=%fused_computation.34 | loop fusion | flops 5602176 | bytes 5315328 | tf_op jit(solution)/shard_map/reduce_sum | solution.py:77
  251.8 0.5 all-gather.4.cloned.1.call-update
  252.6 11.9 %all_gather.14 = bf16[1,32,36,4]{2,1,0,3:T(8,128)(2,1)S(1)} all-gather(bf16[1,32,36,1]{2,1,0,3:T(8,128)(2,1)S(1)} %bitcast.97), channel_id=1, replica_groups=mesh['expert'=32,'dp'=4] {'dp'}, dimensions={3}, use_global_device_ids=true | all-gather | bytes 11520 | tf_op jit(solution)/shard_map/all_gather | solution.py:82
  264.5 0.6 copy.68
  265.2 7.1 %all-to-all-start.4 = ((bf16[32,36,4]{1,2,0:T(4,128)(2,1)}), bf16[32,36,4]{1,2,0:T(4,128)(2,1)S(1)}, u32[]{:S(2)}, u32[]{:S(2)}) async-start(bf16[32,36,4]{1,2,0:T(4,128)(2,1)} %copy.68), calls=%async_computation.7 | async-start | bytes 65536 | tf_op jit(solution)/shard_map/all_to_all | solution.py:106
  272.4 0.1 copy.63
  272.5 0.4 all-gather.8.cloned.1.call-update
  272.9 6.8 %all-to-all-done.4 = bf16[32,36,4]{1,2,0:T(4,128)(2,1)S(1)} async-done(((bf16[32,36,4]{1,2,0:T(4,128)(2,1)}), bf16[32,36,4]{1,2,0:T(4,128)(2,1)S(1)}, u32[]{:S(2)}, u32[]{:S(2)}) %all-to-all-start.4) | async-done | bytes 9248 | tf_op jit(solution)/shard_map/all_to_all | solution.py:106
  279.7 0.1 all_to_all.39
  279.8 0.2 copy.70
  280.1 3.2 gather_fusion.1
  283.3 0.3 convert_reduce_fusion
  283.7 0.7 copy.71
  284.4 6.2 %all-gather.6.cloned.1.call-done = bf16[1,32,36,1024]{3,2,1,0:T(8,128)(2,1)} async-done(((bf16[1,32,36,256]{3,2,1,0:T(8,128)(2,1)}), bf16[1,32,36,1024]{3,2,1,0:T(8,128)(2,1)}) %all-gather.6.cloned.1.call-update) | async-done | bytes 2359312 | tf_op jit(solution)/shard_map/all_gather | solution.py:81
  290.6 6.4 %fusion.5 = f32[32,36,1024]{2,1,0:T(8,128)} fusion(bf16[1,32,36,1024]{3,2,1,0:T(8,128)(2,1)} %all-gather.6.cloned.1.call-done, bf16[1,1024,1024]{2,1,0:T(8,128)(2,1)S(1)} %copy-done), kind=kOutput, calls=%fused_computation.13 | convolution fusion | flops 2415919104 | bytes 9175040 | tf_op jit(solution)/shard_map/escf,edf->secd/dot_general | solution.py:87
  297.0 35.6 %all-gather.4.cloned.1.call-done = bf16[1,32,36,1024]{3,2,1,0:T(8,128)(2,1)} async-done(((bf16[1,32,36,256]{3,2,1,0:T(8,128)(2,1)}), bf16[1,32,36,1024]{3,2,1,0:T(8,128)(2,1)}) %all-gather.4.cloned.1.call-update) | async-done | bytes 2359312 | tf_op jit(solution)/shard_map/all_gather | solution.py:80
  332.6 8.3 %add_convert_fusion = bf16[32,36,1024]{2,1,0:T(8,128)(2,1)} fusion(f32[32,36,1024]{2,1,0:T(8,128)} %fusion.5, bf16[1,1024,1024]{2,1,0:T(8,128)(2,1)} %param.11, bf16[1,32,36,1024]{3,2,1,0:T(8,128)(2,1)} %all-gather.4.cloned.1.call-done), kind=kOutput, calls=%fused_computation.2 | convolution fusion | flops 2418278400 | bytes 11534336 | tf_op jit(solution)/shard_map/escf,edf->secd/dot_general | solution.py:84
  340.9 7.4 %all-to-all-start.3 = ((bf16[32,36,1024]{2,1,0:T(8,128)(2,1)}), bf16[32,36,1024]{2,1,0:T(8,128)(2,1)}, u32[]{:S(2)}, u32[]{:S(2)}) async-start(bf16[32,36,1024]{2,1,0:T(8,128)(2,1)} %add_convert_fusion), calls=%async_computation.6 | async-start | bytes 5242880 | tf_op jit(solution)/shard_map/all_to_all | solution.py:105
  348.4 7.7 %fusion.12 = f32[1,1024,1024]{2,1,0:T(8,128)} fusion(bf16[32,36,1024]{2,1,0:T(8,128)(2,1)} %copy-done.2, bf16[1,32,36,1024]{3,2,1,0:T(8,128)(2,1)} %all-gather.4.cloned.1.call-done), kind=kOutput, calls=%fused_computation.23 | convolution fusion | flops 2415919104 | bytes 8912896 | tf_op jit(solution)/shard_map/secd,escf->edf/dot_general | solution.py:97
  356.0 4.5 %fusion.15 = f32[1,1024,1024]{2,1,0:T(8,128)} fusion(bf16[32,36,1024]{2,1,0:T(8,128)(2,1)S(1)} %copy-done.3, bf16[1,32,36,1024]{3,2,1,0:T(8,128)(2,1)S(1)} %copy-done.8), kind=kOutput, calls=%fused_computation.24 | convolution fusion | flops 2415919104 | bytes 8912896 | tf_op jit(solution)/shard_map/secd,escf->edf/dot_general | solution.py:100
  360.5 14.1 %all-gather.8.cloned.1.call-done = bf16[1,32,36,1024]{3,2,1,0:T(8,128)(2,1)} async-done(((bf16[1,32,36,256]{3,2,1,0:T(8,128)(2,1)}), bf16[1,32,36,1024]{3,2,1,0:T(8,128)(2,1)}) %all-gather.8.cloned.1.call-update) | async-done | bytes 2359312 | tf_op jit(solution)/shard_map/all_gather | solution.py:79
  374.6 7.5 %fusion.18 = f32[1,1024,1024]{2,1,0:T(8,128)} fusion(bf16[32,36,1024]{2,1,0:T(8,128)(2,1)} %copy-done.4, bf16[1,32,36,1024]{3,2,1,0:T(8,128)(2,1)} %all-gather.8.cloned.1.call-done, bf16[32,36]{1,0:T(8,128)(2,1)S(1)} %get-tuple-element.37), kind=kOutput, calls=%fused_computation.25 | convolution fusion | flops 2417098752 | bytes 8915200 | tf_op jit(solution)/shard_map/escf,secd->efd/dot_general | solution.py:94
  382.1 2.0 all-to-all-done.3
  384.2 4.1 %all_to_all.36 = bf16[1152,1024]{1,0:T(8,128)(2,1)} reshape(bf16[32,36,1024]{2,1,0:T(8,128)(2,1)} %all-to-all-done.3) | data formatting | bytes 4718592 | tf_op jit(solution)/shard_map/all_to_all | solution.py:105
  388.2 8.1 %gather_fusion = bf16[1024,1024]{1,0:T(8,128)(2,1)} fusion(bf16[1152,1024]{1,0:T(8,128)(2,1)} %all_to_all.36, s32[1024]{0:T(1024)S(1)} %broadcast_clamp_fusion), kind=kCustom, calls=%fused_computation | custom fusion | bytes 4198400 | tf_op jit(solution)/shard_map/jit(_take)/gather | solution.py:108
  396.4 3.4 fusion.23
  (50 shorter events, 1.7 us)
Async XLA Ops:
  7.2 66.1 %copy-start = (bf16[1,1024,1024]{2,1,0:T(8,128)(2,1)S(1)}, bf16[1,1024,1024]{2,1,0:T(8,128)(2,1)}, u32[]{:S(2)}) copy-start(bf16[1,1024,1024]{2,1,0:T(8,128)(2,1)} %param.12) | copy-start | bytes 6291460
  7.2 142.6 %reduce-scatter.6.cloned.1.call-start = ((), (), s32[]{:S(2)}) async-start(), calls=%async_computation.9 | async-start | bytes 6553600 | tf_op jit(solution)/shard_map/reduce_scatter | solution.py:71
  71.7 1.5 copy-start.2
  77.9 112.0 %reduce-scatter.8.cloned.1.call-start = ((), (), s32[]{:S(2)}) async-start(), calls=%async_computation.10 | async-start | bytes 6553600 | tf_op jit(solution)/shard_map/reduce_scatter | solution.py:70
  85.5 1.0 copy-start.5
  85.5 162.0 %reduce-scatter.4.cloned.1.call-start = ((), (), s32[]{:S(2)}) async-start(), calls=%async_computation.8 | async-start | bytes 6553600 | tf_op jit(solution)/shard_map/reduce_scatter | solution.py:72
  92.8 39.9 %copy-start.9 = (bf16[1,1024,1024]{2,1,0:T(8,128)(2,1)S(1)}, bf16[1,1024,1024]{2,1,0:T(8,128)(2,1)}, u32[]{:S(2)}) copy-start(bf16[1,1024,1024]{2,1,0:T(8,128)(2,1)} %param.13) | copy-start | bytes 6291460
  131.2 1.5 copy-start.4
  137.4 0.7 copy-start.7
  137.4 153.2 %all-gather.6.cloned.1.call-start = ((), (), s32[]{:S(2)}) async-start(), calls=%async_computation.12 | async-start | bytes 3276800 | tf_op jit(solution)/shard_map/all_gather | solution.py:81
  247.5 4.9 %copy-start.6 = (s32[128,8]{0,1:T(8,128)S(1)}, s32[128,8]{0,1:T(8,128)}, u32[]{:S(2)}) copy-start(s32[128,8]{0,1:T(8,128)} %param.10) | copy-start | bytes 12292
  251.8 80.8 %all-gather.4.cloned.1.call-start = ((), (), s32[]{:S(2)}) async-start(), calls=%async_computation.11 | async-start | bytes 3276800 | tf_op jit(solution)/shard_map/all_gather | solution.py:80
  265.2 14.5 %all-to-all-start.4 = ((bf16[32,36,4]{1,2,0:T(4,128)(2,1)}), bf16[32,36,4]{1,2,0:T(4,128)(2,1)S(1)}, u32[]{:S(2)}, u32[]{:S(2)}) async-start(bf16[32,36,4]{1,2,0:T(4,128)(2,1)} %copy.68), calls=%async_computation.7 | async-start | bytes 65536 | tf_op jit(solution)/shard_map/all_to_all | solution.py:106
  272.3 102.3 %all-gather.8.cloned.1.call-start = ((), (), s32[]{:S(2)}) async-start(), calls=%async_computation.13 | async-start | bytes 3276800 | tf_op jit(solution)/shard_map/all_gather | solution.py:79
  340.9 43.2 %all-to-all-start.3 = ((bf16[32,36,1024]{2,1,0:T(8,128)(2,1)}), bf16[32,36,1024]{2,1,0:T(8,128)(2,1)}, u32[]{:S(2)}, u32[]{:S(2)}) async-start(bf16[32,36,1024]{2,1,0:T(8,128)(2,1)} %add_convert_fusion), calls=%async_computation.6 | async-start | bytes 5242880 | tf_op jit(solution)/shard_map/all_to_all | solution.py:105
  348.3 7.7 %copy-start.3 = (bf16[32,36,1024]{2,1,0:T(8,128)(2,1)S(1)}, bf16[32,36,1024]{2,1,0:T(8,128)(2,1)}, u32[]{:S(2)}) copy-start(bf16[32,36,1024]{2,1,0:T(8,128)(2,1)} %copy-done.2) | copy-start | bytes 7077892
  348.4 7.7 %copy-start.8 = (bf16[1,32,36,1024]{3,2,1,0:T(8,128)(2,1)S(1)}, bf16[1,32,36,1024]{3,2,1,0:T(8,128)(2,1)}, u32[]{:S(2)}) copy-start(bf16[1,32,36,1024]{3,2,1,0:T(8,128)(2,1)} %all-gather.6.cloned.1.call-done) | copy-start | bytes 7077892
  388.2 11.5 %copy-start.1 = (bf16[1,1024,1024]{2,1,0:T(8,128)(2,1)S(1)}, bf16[1,1024,1024]{2,1,0:T(8,128)(2,1)}, u32[]{:S(2)}) copy-start(bf16[1,1024,1024]{2,1,0:T(8,128)(2,1)} %param.12) | copy-start | bytes 6291460
Sparse Core Ops, SparseCore 0:
  78.0 54.2 reduce-scatter.5
  134.7 55.1 reduce-scatter.7
  192.3 55.1 reduce-scatter.3
  251.9 38.6 all-gather.5
  292.7 39.8 all-gather.3
  334.7 39.8 all-gather.7
where the time goes:
time: 408 us; the launch traced here: 407 us
  waiting for transfers between devices  163 us (40%)
  blocking collectives  103 us (25%)
  matrix products  56.6 us (14%)
  local copies, waits for them, and re-layouts  32.1 us (8%)
  other arithmetic  22.7 us (6%)
  starting transfers between devices  14.8 us (4%)
  between operations  14.3 us (4%)
    reduce_scatter x1, waiting for transfers between devices, shards(): lax.psum_scatter(back_part, 'dp', scatter_dimension=3, tiled=True)  57.6 us
    all_to_all x1, blocking collectives, shards(): lax.all_to_all(x_send, 'expert', split_axis=0, concat_axis=0, tiled=True)  41.6 us
    reduce_scatter x1, waiting for transfers between devices, shards(): lax.psum_scatter(gate_part, 'dp', scatter_dimension=3, tiled=True)  40.1 us
    all_to_all x1, blocking collectives, shards(): lax.all_to_all(dy_send, 'expert', split_axis=0, concat_axis=0, tiled=True)  38.4 us
    all_gather x1, waiting for transfers between devices, shards(): lax.all_gather(grad_gate_pre, 'dp', axis=3, tiled=True)  35.6 us
    all_gather x1, waiting for transfers between devices, shards(): lax.all_gather(hidden, 'dp', axis=3, tiled=True)  14.1 us
    all_gather x1, blocking collectives, shards(): lax.all_gather(block_sum, 'dp', axis=3, tiled=True)  11.9 us
    all_to_all x1, blocking collectives, shards(): lax.all_to_all(g_send, 'expert', split_axis=0, concat_axis=0, tiled=True)  10.7 us
  transfers between devices with their start and end apart: 8, of which 7 were waited for; matrix products, arithmetic and copies ran while one was open for 14% of the time, Pallas kernels for 0%

commit v1 on v0

--- a/solution.py
+++ b/solution.py
@@ -6,6 +6,19 @@
 TOP = 8
 EXPERTS = 32
 CAP = 36
+
+
+def collect(shard, axis, dim):
+    ways = lax.axis_size(axis)
+    up = [(d, (d + 1) % ways) for d in range(ways)]
+    down = [(d, (d - 1) % ways) for d in range(ways)]
+    earlier, later = ([shard], [shard])
+    for _ in range(ways // 2):
+        earlier.append(lax.ppermute(earlier[-1], axis, up))
+    for _ in range((ways - 1) // 2):
+        later.append(lax.ppermute(later[-1], axis, down))
+    line = jnp.concatenate([*earlier[::-1], *later[1:]], axis=dim)
+    return jnp.roll(line, (lax.axis_index(axis) - ways // 2) * shard.shape[dim], axis=dim)
 
 
 def local_slots(expert_ids):
@@ -79,7 +92,7 @@
         lax.all_gather(hidden, "dp", axis=3, tiled=True),
         lax.all_gather(grad_gate_pre, "dp", axis=3, tiled=True),
         lax.all_gather(grad_up_pre, "dp", axis=3, tiled=True),
-        lax.all_gather(block_sum, "dp", axis=3, tiled=True),
+        collect(block_sum, "dp", 3),
     )
     input_terms = jnp.einsum(
         "escf,edf->secd", gate_grad_all, gate_weight, preferred_element_type=jnp.float32

time: 408 us -> 408 us (level)
  blocking collectives: 103 us -> 90.8 us
  waiting for transfers between devices: 163 us -> 172 us
    all_gather x1 -> x0, blocking collectives: 11.9 us -> none  [shards(): lax.all_gather(block_sum, 'dp', axis=3, tiled=True)]
    ppermute x0 -> x3, waiting for transfers between devices: none -> 6 us  [the longest x2 6 us: collect(): earlier.append(lax.ppermute(earlier[-1], axis, up))]
  transfers between devices with their start and end apart: 8 -> 11, of which waited for: 7 -> 9; matrix products, arithmetic and copies ran while one was open for 14% -> 14% of each run, Pallas kernels for 0% -> 0%
where the time goes in v1:
time: 408 us; the launch traced here: 407 us
  waiting for transfers between devices  172 us (42%)
  blocking collectives  90.8 us (22%)
  matrix products  56.6 us (14%)
  local copies, waits for them, and re-layouts  32.1 us (8%)
  other arithmetic  22.7 us (6%)
  starting transfers between devices  18.3 us (4%)
  between operations  14.3 us (4%)
    reduce_scatter x1, waiting for transfers between devices, shards(): lax.psum_scatter(back_part, 'dp', scatter_dimension=3, tiled=True)  57.6 us
    all_to_all x1, blocking collectives, shards(): lax.all_to_all(x_send, 'expert', split_axis=0, concat_axis=0, tiled=True)  41.6 us
    reduce_scatter x1, waiting for transfers between devices, shards(): lax.psum_scatter(gate_part, 'dp', scatter_dimension=3, tiled=True)  40.1 us
    all_to_all x1, blocking collectives, shards(): lax.all_to_all(dy_send, 'expert', split_axis=0, concat_axis=0, tiled=True)  38.4 us
    all_gather x1, waiting for transfers between devices, shards(): lax.all_gather(grad_gate_pre, 'dp', axis=3, tiled=True)  35.6 us
    all_gather x1, waiting for transfers between devices, shards(): lax.all_gather(hidden, 'dp', axis=3, tiled=True)  14.1 us
    all_to_all x1, blocking collectives, shards(): lax.all_to_all(g_send, 'expert', split_axis=0, concat_axis=0, tiled=True)  10.7 us
    another operation x2, other arithmetic  9.04 us
  transfers between devices with their start and end apart: 11, of which 9 were waited for; matrix products, arithmetic and copies ran while one was open for 14% of the time, Pallas kernels for 0%

profile of v1, /device:TPU:0, one launch (start us, length us, event | category | flops | bytes accessed | tf_op | source)
XLA Modules:
  0.0 406.6 jit_solution(2140627445903197826)
XLA Ops:
  7.2 0.9 copy.54
  8.4 9.0 %reduce-window.6 = s32[32,8,128]{2,1,0:T(8,128)S(1)} reduce-window(s32[32,8,128]{2,1,0:T(8,128)S(1)} %fusion.37, s32[]{:T(128)} %constant.60.clone.1), window={size=1x1x128 pad=0_0x0_0x127_0}, to_apply=%region_0.0 | reduce-window | flops 4161536 | bytes 262148 | tf_op jit(solution)/shard_map/reduce-window
  18.0 0.7 compare_and_fusion.1
  18.7 4.2 %fusion = pred[1152,128]{1,0:T(8,128)(4,1)S(1)} fusion(s32[128,8]{0,1:T(8,128)S(1)} %get-tuple-element.35), kind=kLoop, calls=%fused_computation.6 | loop fusion | flops 2211840 | bytes 151552 | tf_op jit(solution)/shard_map/reduce_or | solution.py:38
  22.9 3.1 convolution_convert_fusion
  26.0 4.1 all_to_all.33
  30.1 41.6 %all_to_all.45 = bf16[32,36,1024]{2,1,0:T(8,128)(2,1)S(1)} all-to-all(bf16[32,36,1024]{2,1,0:T(8,128)(2,1)} %all_to_all.33), channel_id=1, replica_groups=mesh['expert'=32,'dp'=4] {'expert'}, dimensions={0} | all-to-all | bytes 4718592 | tf_op jit(solution)/shard_map/all_to_all | solution.py:67
  71.7 1.5 copy-done.2
  73.2 4.6 %convolution_bitcast_fusion.1 = f32[1,32,36,1024]{3,2,1,0:T(8,128)} fusion(bf16[32,36,1024]{2,1,0:T(8,128)(2,1)S(1)} %all_to_all.45, bf16[1,1024,1024]{2,1,0:T(8,128)(2,1)S(1)} %copy-done), kind=kOutput, calls=%fused_computation.21 | convolution fusion | flops 2415919104 | bytes 9175040 | tf_op jit(solution)/shard_map/secd,edf->escf/dot_general | solution.py:78
  77.9 7.6 %convolution_bitcast_fusion = f32[1,32,36,1024]{3,2,1,0:T(8,128)} fusion(bf16[32,36,1024]{2,1,0:T(8,128)(2,1)} %copy-done.2, bf16[1,1024,1024]{2,1,0:T(8,128)(2,1)} %param.11), kind=kOutput, calls=%fused_computation.20 | convolution fusion | flops 2415919104 | bytes 9175040 | tf_op jit(solution)/shard_map/secd,edf->escf/dot_general | solution.py:75
  85.6 0.9 copy-done.5
  86.5 2.2 convolution_convert_fusion.1
  88.7 4.1 all_to_all.31
  92.8 38.4 %all_to_all.46 = bf16[32,36,1024]{2,1,0:T(8,128)(2,1)S(1)} all-to-all(bf16[32,36,1024]{2,1,0:T(8,128)(2,1)} %all_to_all.31), channel_id=1, replica_groups=mesh['expert'=32,'dp'=4] {'expert'}, dimensions={0} | all-to-all | bytes 4718592 | tf_op jit(solution)/shard_map/all_to_all | solution.py:68
  131.2 1.5 copy-done.4
  132.7 4.7 %convolution_bitcast_fusion.2 = f32[1,32,36,1024]{3,2,1,0:T(8,128)} fusion(bf16[32,36,1024]{2,1,0:T(8,128)(2,1)S(1)} %all_to_all.46, bf16[1,1024,1024]{2,1,0:T(8,128)(2,1)S(1)} %copy-done.9), kind=kOutput, calls=%fused_computation.22 | convolution fusion | flops 2415919104 | bytes 9175040 | tf_op jit(solution)/shard_map/secd,efd->escf/dot_general | solution.py:79
  137.5 0.6 copy-done.7
  138.3 0.6 select_reduce_fusion
  139.0 10.7 %all_to_all.47 = bf16[32,36,1]{1,2,0:T(2,128)(2,1)S(1)} all-to-all(bf16[32,36,1]{1,2,0:T(2,128)(2,1)S(1)} %convert_element_type.99), channel_id=1, replica_groups=mesh['expert'=32,'dp'=4] {'expert'}, dimensions={0} | all-to-all | bytes 4608 | tf_op jit(solution)/shard_map/all_to_all | solution.py:69
  149.7 40.1 %reduce-scatter.8.cloned.1.call-done = f32[1,32,36,256]{3,2,1,0:T(8,128)} async-done(((f32[1,32,36,1024]{3,2,1,0:T(8,128)}), f32[1,32,36,256]{3,2,1,0:T(8,128)}) %reduce-scatter.8.cloned.1.call-update) | async-done | bytes 1179664 | tf_op jit(solution)/shard_map/reduce_scatter | solution.py:83
  189.9 57.6 %reduce-scatter.4.cloned.1.call-done = f32[1,32,36,256]{3,2,1,0:T(8,128)} async-done(((f32[1,32,36,1024]{3,2,1,0:T(8,128)}), f32[1,32,36,256]{3,2,1,0:T(8,128)}) %reduce-scatter.4.cloned.1.call-update) | async-done | bytes 1179664 | tf_op jit(solution)/shard_map/reduce_scatter | solution.py:85
  247.5 4.3 %multiply_reduce_fusion = (bf16[32,36]{1,0:T(8,128)(2,1)S(1)}, bf16[1,32,36,256]{3,2,1,0:T(8,128)(2,1)}, bf16[1,32,36,256]{3,2,1,0:T(8,128)(2,1)}, bf16[1,32,36,256]{3,2,1,0:T(8,128)(2,1)}) fusion(f32[1,32,36,256]{3,2,1,0:T(8,128)} %reduce-scatter.4.cloned.1.call-done, f32[1,32,36,256]{3,2,1,0:T(8,128)} %reduce-scatter.6.cloned.1.call-done, ...), kind=kLoop, calls=%fused_computation.34 | loop fusion | flops 5602176 | bytes 5315328 | tf_op jit(solution)/shard_map/reduce_sum | solution.py:90
  251.8 0.5 all-gather.4.cloned.1.call-update
  252.4 0.2 collective-permute-start
  252.8 4.5 %collective-permute-done = bf16[1,32,36,1]{2,1,3,0:T(8,128)(2,1)S(1)} collective-permute-done((bf16[1,32,36,1]{2,1,3,0:T(8,128)(2,1)S(1)}, bf16[1,32,36,1]{2,1,3,0:T(8,128)(2,1)S(1)}, u32[]{:S(2)}, u32[]{:S(2)}) %collective-permute-start) | collective-permute-done | bytes 2336 | tf_op jit(solution)/shard_map/ppermute | solution.py:17
  257.4 3.3 collective-permute-start.2
  260.7 1.5 collective-permute-done.1
  262.3 0.6 copy.63
  262.9 7.1 %all-to-all-start.4 = ((bf16[32,36,4]{1,2,0:T(4,128)(2,1)}), bf16[32,36,4]{1,2,0:T(4,128)(2,1)S(1)}, u32[]{:S(2)}, u32[]{:S(2)}) async-start(bf16[32,36,4]{1,2,0:T(4,128)(2,1)} %copy.63), calls=%async_computation.7 | async-start | bytes 65536 | tf_op jit(solution)/shard_map/all_to_all | solution.py:119
  270.2 0.4 all-gather.8.cloned.1.call-update
  270.6 6.8 %all-to-all-done.4 = bf16[32,36,4]{1,2,0:T(4,128)(2,1)S(1)} async-done(((bf16[32,36,4]{1,2,0:T(4,128)(2,1)}), bf16[32,36,4]{1,2,0:T(4,128)(2,1)S(1)}, u32[]{:S(2)}, u32[]{:S(2)}) %all-to-all-start.4) | async-done | bytes 9248 | tf_op jit(solution)/shard_map/all_to_all | solution.py:119
  277.6 0.2 copy.65
  277.8 3.2 gather_fusion.1
  281.1 0.3 convert_reduce_fusion
  281.4 0.7 copy.66
  282.1 8.5 %all-gather.6.cloned.1.call-done = bf16[1,32,36,1024]{3,2,1,0:T(8,128)(2,1)} async-done(((bf16[1,32,36,256]{3,2,1,0:T(8,128)(2,1)}), bf16[1,32,36,1024]{3,2,1,0:T(8,128)(2,1)}) %all-gather.6.cloned.1.call-update) | async-done | bytes 2359312 | tf_op jit(solution)/shard_map/all_gather | solution.py:94
  290.6 6.4 %fusion.5 = f32[32,36,1024]{2,1,0:T(8,128)} fusion(bf16[1,32,36,1024]{3,2,1,0:T(8,128)(2,1)} %all-gather.6.cloned.1.call-done, bf16[1,1024,1024]{2,1,0:T(8,128)(2,1)S(1)} %copy-done), kind=kOutput, calls=%fused_computation.13 | convolution fusion | flops 2415919104 | bytes 9175040 | tf_op jit(solution)/shard_map/escf,edf->secd/dot_general | solution.py:100
  297.0 35.6 %all-gather.4.cloned.1.call-done = bf16[1,32,36,1024]{3,2,1,0:T(8,128)(2,1)} async-done(((bf16[1,32,36,256]{3,2,1,0:T(8,128)(2,1)}), bf16[1,32,36,1024]{3,2,1,0:T(8,128)(2,1)}) %all-gather.4.cloned.1.call-update) | async-done | bytes 2359312 | tf_op jit(solution)/shard_map/all_gather | solution.py:93
  332.6 8.3 %add_convert_fusion = bf16[32,36,1024]{2,1,0:T(8,128)(2,1)} fusion(f32[32,36,1024]{2,1,0:T(8,128)} %fusion.5, bf16[1,1024,1024]{2,1,0:T(8,128)(2,1)} %param.11, bf16[1,32,36,1024]{3,2,1,0:T(8,128)(2,1)} %all-gather.4.cloned.1.call-done), kind=kOutput, calls=%fused_computation.2 | convolution fusion | flops 2418278400 | bytes 11534336 | tf_op jit(solution)/shard_map/escf,edf->secd/dot_general | solution.py:97
  340.9 7.4 %all-to-all-start.3 = ((bf16[32,36,1024]{2,1,0:T(8,128)(2,1)}), bf16[32,36,1024]{2,1,0:T(8,128)(2,1)}, u32[]{:S(2)}, u32[]{:S(2)}) async-start(bf16[32,36,1024]{2,1,0:T(8,128)(2,1)} %add_convert_fusion), calls=%async_computation.6 | async-start | bytes 5242880 | tf_op jit(solution)/shard_map/all_to_all | solution.py:118
  348.4 7.7 %fusion.12 = f32[1,1024,1024]{2,1,0:T(8,128)} fusion(bf16[32,36,1024]{2,1,0:T(8,128)(2,1)} %copy-done.2, bf16[1,32,36,1024]{3,2,1,0:T(8,128)(2,1)} %all-gather.4.cloned.1.call-done), kind=kOutput, calls=%fused_computation.23 | convolution fusion | flops 2415919104 | bytes 8912896 | tf_op jit(solution)/shard_map/secd,escf->edf/dot_general | solution.py:110
  356.0 4.5 %fusion.15 = f32[1,1024,1024]{2,1,0:T(8,128)} fusion(bf16[32,36,1024]{2,1,0:T(8,128)(2,1)S(1)} %copy-done.3, bf16[1,32,36,1024]{3,2,1,0:T(8,128)(2,1)S(1)} %copy-done.8), kind=kOutput, calls=%fused_computation.24 | convolution fusion | flops 2415919104 | bytes 8912896 | tf_op jit(solution)/shard_map/secd,escf->edf/dot_general | solution.py:113
  360.5 14.1 %all-gather.8.cloned.1.call-done = bf16[1,32,36,1024]{3,2,1,0:T(8,128)(2,1)} async-done(((bf16[1,32,36,256]{3,2,1,0:T(8,128)(2,1)}), bf16[1,32,36,1024]{3,2,1,0:T(8,128)(2,1)}) %all-gather.8.cloned.1.call-update) | async-done | bytes 2359312 | tf_op jit(solution)/shard_map/all_gather | solution.py:92
  374.6 7.5 %fusion.18 = f32[1,1024,1024]{2,1,0:T(8,128)} fusion(bf16[32,36,1024]{2,1,0:T(8,128)(2,1)} %copy-done.4, bf16[1,32,36,1024]{3,2,1,0:T(8,128)(2,1)} %all-gather.8.cloned.1.call-done, bf16[32,36]{1,0:T(8,128)(2,1)S(1)} %get-tuple-element.37), kind=kOutput, calls=%fused_computation.25 | convolution fusion | flops 2417098752 | bytes 8915200 | tf_op jit(solution)/shard_map/escf,secd->efd/dot_general | solution.py:107
  382.1 2.0 all-to-all-done.3
  384.2 4.1 %all_to_all.36 = bf16[1152,1024]{1,0:T(8,128)(2,1)} reshape(bf16[32,36,1024]{2,1,0:T(8,128)(2,1)} %all-to-all-done.3) | data formatting | bytes 4718592 | tf_op jit(solution)/shard_map/all_to_all | solution.py:118
  388.3 8.1 %gather_fusion = bf16[1024,1024]{1,0:T(8,128)(2,1)} fusion(bf16[1152,1024]{1,0:T(8,128)(2,1)} %all_to_all.36, s32[1024]{0:T(1024)S(1)} %broadcast_clamp_fusion), kind=kCustom, calls=%fused_computation | custom fusion | bytes 4198400 | tf_op jit(solution)/shard_map/jit(_take)/gather | solution.py:121
  396.4 3.4 fusion.23
  (64 shorter events, 2.1 us)
Async XLA Ops:
  7.2 66.1 %copy-start = (bf16[1,1024,1024]{2,1,0:T(8,128)(2,1)S(1)}, bf16[1,1024,1024]{2,1,0:T(8,128)(2,1)}, u32[]{:S(2)}) copy-start(bf16[1,1024,1024]{2,1,0:T(8,128)(2,1)} %param.12) | copy-start | bytes 6291460
  7.2 142.6 %reduce-scatter.6.cloned.1.call-start = ((), (), s32[]{:S(2)}) async-start(), calls=%async_computation.9 | async-start | bytes 6553600 | tf_op jit(solution)/shard_map/reduce_scatter | solution.py:84
  71.7 1.5 copy-start.2
  77.9 112.0 %reduce-scatter.8.cloned.1.call-start = ((), (), s32[]{:S(2)}) async-start(), calls=%async_computation.10 | async-start | bytes 6553600 | tf_op jit(solution)/shard_map/reduce_scatter | solution.py:83
  85.5 1.0 copy-start.5
  85.5 162.0 %reduce-scatter.4.cloned.1.call-start = ((), (), s32[]{:S(2)}) async-start(), calls=%async_computation.8 | async-start | bytes 6553600 | tf_op jit(solution)/shard_map/reduce_scatter | solution.py:85
  92.8 39.9 %copy-start.9 = (bf16[1,1024,1024]{2,1,0:T(8,128)(2,1)S(1)}, bf16[1,1024,1024]{2,1,0:T(8,128)(2,1)}, u32[]{:S(2)}) copy-start(bf16[1,1024,1024]{2,1,0:T(8,128)(2,1)} %param.13) | copy-start | bytes 6291460
  131.2 1.5 copy-start.4
  137.4 0.7 copy-start.7
  137.4 153.1 %all-gather.6.cloned.1.call-start = ((), (), s32[]{:S(2)}) async-start(), calls=%async_computation.12 | async-start | bytes 3276800 | tf_op jit(solution)/shard_map/all_gather | solution.py:94
  247.5 5.1 %copy-start.6 = (s32[128,8]{0,1:T(8,128)S(1)}, s32[128,8]{0,1:T(8,128)}, u32[]{:S(2)}) copy-start(s32[128,8]{0,1:T(8,128)} %param.10) | copy-start | bytes 12292
  251.8 80.8 %all-gather.4.cloned.1.call-start = ((), (), s32[]{:S(2)}) async-start(), calls=%async_computation.11 | async-start | bytes 3276800 | tf_op jit(solution)/shard_map/all_gather | solution.py:93
  252.4 4.9 %collective-permute-start = (bf16[1,32,36,1]{2,1,3,0:T(8,128)(2,1)S(1)}, bf16[1,32,36,1]{2,1,3,0:T(8,128)(2,1)S(1)}, u32[]{:S(2)}, u32[]{:S(2)}) collective-permute-start(bf16[1,32,36,1]{2,1,3,0:T(8,128)(2,1)S(1)} %bitcast.96), channel_id=1, source_target_pairs={{0,1},{1,2},{2,3},{3,0},{4,5},{5,6},{6,7},{7,4},{8,9},{9,10},{10,1... | collective-permute-start | bytes 6920 | tf_op jit(solution)/shard_map/ppermute | solution.py:17
  257.3 4.9 %collective-permute-start.1 = (bf16[1,32,36,1]{2,1,3,0:T(8,128)(2,1)S(1)}, bf16[1,32,36,1]{2,1,3,0:T(8,128)(2,1)S(1)}, u32[]{:S(2)}, u32[]{:S(2)}) collective-permute-start(bf16[1,32,36,1]{2,1,3,0:T(8,128)(2,1)S(1)} %collective-permute-done), channel_id=1, source_target_pairs={{0,1},{1,2},{2,3},{3,0},{4,5},{5,6},{6,7},{7,4},{8,9},{9,10},{10,1... | collective-permute-start | bytes 6920 | tf_op jit(solution)/shard_map/ppermute | solution.py:17
  257.4 4.8 %collective-permute-start.2 = (bf16[1,32,36,1]{2,1,3,0:T(8,128)(2,1)S(1)}, bf16[1,32,36,1]{2,1,3,0:T(8,128)(2,1)S(1)}, u32[]{:S(2)}, u32[]{:S(2)}) collective-permute-start(bf16[1,32,36,1]{2,1,3,0:T(8,128)(2,1)S(1)} %bitcast.97), channel_id=1, source_target_pairs={{0,3},{1,0},{2,1},{3,2},{4,7},{5,4},{6,5},{7,6},{8,11},{9,8},{10,9... | collective-permute-start | bytes 6920 | tf_op jit(solution)/shard_map/ppermute | solution.py:19
  262.9 14.5 %all-to-all-start.4 = ((bf16[32,36,4]{1,2,0:T(4,128)(2,1)}), bf16[32,36,4]{1,2,0:T(4,128)(2,1)S(1)}, u32[]{:S(2)}, u32[]{:S(2)}) async-start(bf16[32,36,4]{1,2,0:T(4,128)(2,1)} %copy.63), calls=%async_computation.7 | async-start | bytes 65536 | tf_op jit(solution)/shard_map/all_to_all | solution.py:119
  270.0 104.6 %all-gather.8.cloned.1.call-start = ((), (), s32[]{:S(2)}) async-start(), calls=%async_computation.13 | async-start | bytes 3276800 | tf_op jit(solution)/shard_map/all_gather | solution.py:92
  340.9 43.3 %all-to-all-start.3 = ((bf16[32,36,1024]{2,1,0:T(8,128)(2,1)}), bf16[32,36,1024]{2,1,0:T(8,128)(2,1)}, u32[]{:S(2)}, u32[]{:S(2)}) async-start(bf16[32,36,1024]{2,1,0:T(8,128)(2,1)} %add_convert_fusion), calls=%async_computation.6 | async-start | bytes 5242880 | tf_op jit(solution)/shard_map/all_to_all | solution.py:118
  348.4 7.7 %copy-start.3 = (bf16[32,36,1024]{2,1,0:T(8,128)(2,1)S(1)}, bf16[32,36,1024]{2,1,0:T(8,128)(2,1)}, u32[]{:S(2)}) copy-start(bf16[32,36,1024]{2,1,0:T(8,128)(2,1)} %copy-done.2) | copy-start | bytes 7077892
  348.4 7.7 %copy-start.8 = (bf16[1,32,36,1024]{3,2,1,0:T(8,128)(2,1)S(1)}, bf16[1,32,36,1024]{3,2,1,0:T(8,128)(2,1)}, u32[]{:S(2)}) copy-start(bf16[1,32,36,1024]{3,2,1,0:T(8,128)(2,1)} %all-gather.6.cloned.1.call-done) | copy-start | bytes 7077892
  388.3 11.5 %copy-start.1 = (bf16[1,1024,1024]{2,1,0:T(8,128)(2,1)S(1)}, bf16[1,1024,1024]{2,1,0:T(8,128)(2,1)}, u32[]{:S(2)}) copy-start(bf16[1,1024,1024]{2,1,0:T(8,128)(2,1)} %param.12) | copy-start | bytes 6291460
Sparse Core Ops, SparseCore 0:
  78.0 54.2 reduce-scatter.5
  134.7 55.1 reduce-scatter.7
  192.3 55.1 reduce-scatter.3
  251.9 38.6 all-gather.5
  292.7 39.8 all-gather.3
  334.7 39.8 all-gather.7
